TPU v7x, 32 devices: a whole 2x2x4 slice. The times are simulated.
32 devices in a mesh: row: 8 (over z, y), col: 4 (over x, core).
Axes of the slice: x: 2, y: 2, z: 4, core: 2. Of those that a mesh axis runs over, the one named last changes fastest.
Arguments:
- factor: float32 [2, 1024, 1024], P(None, 'row', 'col'), may hold values from -0.125 to 0.125
- lower_inverse: float32 [2, 512, 1024], P(None, None, 'row'), may hold values from -1 to 2
- upper_inverse: float32 [2, 512, 1024], P(None, None, 'row'), may hold values from -1 to 2
- krylov_block: float32 [2, 16, 1024], P(None, None, 'row'), may hold values from -6 to 6
- basis: float32 [2, 64, 1024], P(None, None, 'row'), may hold values from -0.125 to 0.125
Outputs:
- projected: float32 [2, 16, 1024], P(None, None, 'row')
- coefficients: float32 [2, 64, 16], replicated
All inputs are finite; a program needn't handle non-finite values.
Results may differ from a plain program's by a relative error of at most 0.00012.
Values sent between devices are 32-bit elements; how exact they have to be, the bound alone decides.
A program may use at most 64 MiB of HBM per device.

v0:
```python
import jax
import jax.numpy as jnp
from jax import lax
from jax.sharding import PartitionSpec as P


def real_dot(left, right):
    return jnp.dot(left, right, preferred_element_type=jnp.float32, precision=lax.Precision.HIGHEST)


def apply_tile(matrix, vectors):
    real_part = real_dot(vectors[0], matrix[0].T) - real_dot(vectors[1], matrix[1].T)
    imag_part = real_dot(vectors[0], matrix[1].T) + real_dot(vectors[1], matrix[0].T)
    return jnp.stack([real_part, imag_part])


def herm_dot(basis_part, vectors):
    real_part = real_dot(basis_part[0], vectors[0].T) + real_dot(basis_part[1], vectors[1].T)
    imag_part = real_dot(basis_part[0], vectors[1].T) - real_dot(basis_part[1], vectors[0].T)
    return jnp.stack([real_part, imag_part])


def combine(basis_part, coeffs):
    real_part = real_dot(coeffs[0].T, basis_part[0]) - real_dot(coeffs[1].T, basis_part[1])
    imag_part = real_dot(coeffs[0].T, basis_part[1]) + real_dot(coeffs[1].T, basis_part[0])
    return jnp.stack([real_part, imag_part])


def small_product(gram, coeffs):
    real_part = real_dot(gram[0], coeffs[0]) - real_dot(gram[1], coeffs[1])
    imag_part = real_dot(gram[0], coeffs[1]) + real_dot(gram[1], coeffs[0])
    return jnp.stack([real_part, imag_part])


def local(factor, lower_inverse, upper_inverse, krylov_block, basis):
    tile = lower_inverse.shape[1]
    rows_local = factor.shape[1]
    width = factor.shape[2]
    nvec = krylov_block.shape[1]
    share = tile // rows_local
    tiles = lax.axis_size("row") // share
    row_idx = lax.axis_index("row")
    col_idx = lax.axis_index("col")
    own_tile = row_idx // share
    piece_idx = row_idx % share

    def sweep(inverse, pick, backward):
        start = jnp.zeros((2, nvec, tiles * tile), jnp.float32)

        def step(index, current):
            k = tiles - 1 - index if backward else index
            k = jnp.asarray(k).astype(jnp.int32)
            owner = own_tile == k
            cols = lax.dynamic_slice_in_dim(current, col_idx * width, width, 2)
            partial_value = apply_tile(factor, cols)
            given = pick(k)
            summed = lax.psum(partial_value, "col")
            term = apply_tile(inverse, given - summed)
            term = jnp.where(owner, term, jnp.zeros_like(term))
            piece = lax.psum(term, "row")
            return lax.dynamic_update_slice_in_dim(current, piece, k * tile, 2)

        return lax.fori_loop(0, tiles, step, start)

    def pick_forward(k):
        return krylov_block

    solved = sweep(lower_inverse, pick_forward, False)

    def pick_backward(k):
        return lax.dynamic_slice_in_dim(solved, k * tile + piece_idx * rows_local, rows_local, 2)

    solution = sweep(upper_inverse, pick_backward, True)
    own_rows = lax.dynamic_slice_in_dim(solution, row_idx * rows_local, rows_local, 2)
    local_first = herm_dot(basis, own_rows)
    first, gram = lax.psum((local_first, herm_dot(basis, basis)), "row")
    middle = own_rows - combine(basis, first)
    second = first - small_product(gram, first)
    projected = middle - combine(basis, second)
    return (projected, first + second)


def solution(mesh):
    in_specs = (
        P(None, "row", "col"),
        P(None, None, "row"),
        P(None, None, "row"),
        P(None, None, "row"),
        P(None, None, "row"),
    )
    out_specs = (P(None, None, "row"), P())
    return jax.shard_map(local, mesh=mesh, in_specs=in_specs, out_specs=out_specs, check_vma=False)
```

profile of v0, /device:TPU:0, one launch (start us, length us, event | category | flops | bytes accessed | tf_op | source)
XLA Modules:
  0.0 401.9 jit_solution(1856466188070907710)
XLA Ops:
  7.2 0.7 copy-done.5
  7.9 175.2 %while.30 = (s32[]{:T(128)}, f32[2,16,1024]{2,1,0:T(8,128)S(1)}, s32[]{:T(128)}, s32[]{:T(128)}, f32[2,128,256]{2,1,0:T(8,128)}, /*index=5*/f32[2,16,128]{2,1,0:...) while((s32[]{:T(128)}, f32[2,16,1024]{2,1,0:T(8,128)S(1)}, ...), condition=%wide.region_3.4_spmd, body=%wide.region_0.3_spmd.sunk | while | flops 75579392 | bytes 5834029 | solution.py:63
  7.9 1.2 fusion.158
  9.1 1.1 fusion.160
  10.7 12.7 %psum.72 = f32[2,16,128]{2,1,0:T(8,128)S(1)} all-reduce(f32[2,16,128]{2,1,0:T(8,128)S(1)} %pad_maximum_fusion.6), channel_id=1, replica_groups=mesh['row'=8,'col'=4] {'col'}, use_global_device_ids=true, to_apply=%region_1.1 | all-reduce | flops 4096 | bytes 32768 | tf_op jit(solution)/shard_map/while/body/eval_jaxpr/psum | solution.py:57
  23.4 1.3 fusion.164
  25.6 0.6 maximum_select_fusion.4
  26.3 69.7 %all-reduce.4.cloned.1.call-done = f32[2,16,512]{2,1,0:T(8,128)} async-done(((f32[2,16,512]{2,1,0:T(8,128)}), f32[2,16,512]{2,1,0:T(8,128)}) %all-reduce.4.cloned.1.call-update) | async-done | bytes 65552 | tf_op jit(solution)/shard_map/while/body/eval_jaxpr/psum | solution.py:60
  96.0 0.8 constant_dynamic-update-slice_fusion.4
  96.9 1.1 fusion.158
  98.1 1.1 fusion.160
  99.7 10.1 %psum.72 = f32[2,16,128]{2,1,0:T(8,128)S(1)} all-reduce(f32[2,16,128]{2,1,0:T(8,128)S(1)} %pad_maximum_fusion.6), channel_id=1, replica_groups=mesh['row'=8,'col'=4] {'col'}, use_global_device_ids=true, to_apply=%region_1.1 | all-reduce | flops 4096 | bytes 32768 | tf_op jit(solution)/shard_map/while/body/eval_jaxpr/psum | solution.py:57
  109.8 1.3 fusion.164
  112.1 0.6 maximum_select_fusion.4
  112.7 69.5 %all-reduce.4.cloned.1.call-done = f32[2,16,512]{2,1,0:T(8,128)} async-done(((f32[2,16,512]{2,1,0:T(8,128)}), f32[2,16,512]{2,1,0:T(8,128)}) %all-reduce.4.cloned.1.call-update) | async-done | bytes 65552 | tf_op jit(solution)/shard_map/while/body/eval_jaxpr/psum | solution.py:60
  182.2 0.8 constant_dynamic-update-slice_fusion.4
  183.1 170.5 %while.31 = (s32[]{:T(128)}, f32[2,16,1024]{2,1,0:T(8,128)S(1)}, s32[]{:T(128)}, s32[]{:T(128)}, f32[2,16,1024]{2,1,0:T(8,128)S(1)}, /*index=5*/s32[]{:T(128)}, ...) while((s32[]{:T(128)}, f32[2,16,1024]{2,1,0:T(8,128)S(1)}, ...), condition=%wide.region_7.8_spmd, body=%wide.region_4.7_spmd.sunk | while | flops 75579392 | bytes 5834099 | solution.py:63
  183.2 1.1 fusion.174
  184.3 1.1 fusion.176
  185.9 10.1 %psum.74 = f32[2,16,128]{2,1,0:T(8,128)S(1)} all-reduce(f32[2,16,128]{2,1,0:T(8,128)S(1)} %pad_maximum_fusion.7), channel_id=1, replica_groups=mesh['row'=8,'col'=4] {'col'}, use_global_device_ids=true, to_apply=%region_5.5 | all-reduce | flops 4096 | bytes 32768 | tf_op jit(solution)/shard_map/while/body/eval_jaxpr/psum | solution.py:57
  197.4 0.6 maximum_select_fusion.5
  198.0 69.5 %all-reduce.6.cloned.1.call-done = f32[2,16,512]{2,1,0:T(8,128)} async-done(((f32[2,16,512]{2,1,0:T(8,128)}), f32[2,16,512]{2,1,0:T(8,128)}) %all-reduce.6.cloned.1.call-update) | async-done | bytes 65552 | tf_op jit(solution)/shard_map/while/body/eval_jaxpr/psum | solution.py:60
  267.5 0.8 constant_dynamic-update-slice_fusion.5
  268.4 1.1 fusion.174
  269.6 1.1 fusion.176
  271.2 10.1 %psum.74 = f32[2,16,128]{2,1,0:T(8,128)S(1)} all-reduce(f32[2,16,128]{2,1,0:T(8,128)S(1)} %pad_maximum_fusion.7), channel_id=1, replica_groups=mesh['row'=8,'col'=4] {'col'}, use_global_device_ids=true, to_apply=%region_5.5 | all-reduce | flops 4096 | bytes 32768 | tf_op jit(solution)/shard_map/while/body/eval_jaxpr/psum | solution.py:57
  282.6 0.6 maximum_select_fusion.5
  283.3 69.5 %all-reduce.6.cloned.1.call-done = f32[2,16,512]{2,1,0:T(8,128)} async-done(((f32[2,16,512]{2,1,0:T(8,128)}), f32[2,16,512]{2,1,0:T(8,128)}) %all-reduce.6.cloned.1.call-update) | async-done | bytes 65552 | tf_op jit(solution)/shard_map/while/body/eval_jaxpr/psum | solution.py:60
  352.8 0.8 constant_dynamic-update-slice_fusion.5
  355.1 37.1 %all-reduce = (f32[2,64,16]{1,2,0:T(8,128)S(1)}, f32[2,64,64]{2,1,0:T(8,128)S(1)}) all-reduce(f32[2,64,16]{1,2,0:T(8,128)S(1)} %pad_maximum_fusion.3, f32[2,64,64]{2,1,0:T(8,128)S(1)} %pad_maximum_fusion.2), channel_id=1, replica_groups=mesh['row'=8,'col'=4] {'row'}, use_global_device_ids=true, to_apply=%region_8.9 | all-reduce | flops 10240 | bytes 81920 | tf_op jit(solution)/shard_map/psum | solution.py:76
  392.9 0.6 fusion.117
  394.7 0.6 fusion.112
  (81 shorter events, 9.9 us)
Async XLA Ops:
  7.2 0.7 copy-start.5
  7.9 345.7 %copy-start.4 = (f32[2,64,128]{2,1,0:T(8,128)S(1)}, f32[2,64,128]{2,1,0:T(8,128)}, u32[]{:S(2)}) copy-start(f32[2,64,128]{2,1,0:T(8,128)} %param.13) | copy-start | bytes 196612
  7.9 2.3 copy-start
  7.9 88.1 %all-reduce.4.cloned.1.call-start = ((), (), s32[]{:S(2)}) async-start(), calls=%async_computation | async-start | bytes 131072 | tf_op jit(solution)/shard_map/while/body/eval_jaxpr/psum | solution.py:60
  7.9 16.8 %copy-start.2 = (f32[2,512,128]{2,1,0:T(8,128)S(1)}, f32[2,512,128]{2,1,0:T(8,128)}, u32[]{:S(2)}) copy-start(f32[2,512,128]{2,1,0:T(8,128)} %get-tuple-element.529) | copy-start | bytes 1572868 | tf_op jit(solution)/shard_map/while
  96.9 2.4 copy-start
  96.9 85.4 %all-reduce.4.cloned.1.call-start = ((), (), s32[]{:S(2)}) async-start(), calls=%async_computation | async-start | bytes 131072 | tf_op jit(solution)/shard_map/while/body/eval_jaxpr/psum | solution.py:60
  96.9 14.2 %copy-start.2 = (f32[2,512,128]{2,1,0:T(8,128)S(1)}, f32[2,512,128]{2,1,0:T(8,128)}, u32[]{:S(2)}) copy-start(f32[2,512,128]{2,1,0:T(8,128)} %get-tuple-element.529) | copy-start | bytes 1572868 | tf_op jit(solution)/shard_map/while
  183.1 2.4 copy-start.1
  183.1 13.0 %copy-start.3 = (f32[2,512,128]{2,1,0:T(8,128)S(1)}, f32[2,512,128]{2,1,0:T(8,128)}, u32[]{:S(2)}) copy-start(f32[2,512,128]{2,1,0:T(8,128)} %get-tuple-element.568) | copy-start | bytes 1572868 | tf_op jit(solution)/shard_map/while
  183.1 84.4 %all-reduce.6.cloned.1.call-start = ((), (), s32[]{:S(2)}) async-start(), calls=%async_computation.1 | async-start | bytes 131072 | tf_op jit(solution)/shard_map/while/body/eval_jaxpr/psum | solution.py:60
  268.4 2.4 copy-start.1
  268.4 13.0 %copy-start.3 = (f32[2,512,128]{2,1,0:T(8,128)S(1)}, f32[2,512,128]{2,1,0:T(8,128)}, u32[]{:S(2)}) copy-start(f32[2,512,128]{2,1,0:T(8,128)} %get-tuple-element.568) | copy-start | bytes 1572868 | tf_op jit(solution)/shard_map/while
  268.4 84.4 %all-reduce.6.cloned.1.call-start = ((), (), s32[]{:S(2)}) async-start(), calls=%async_computation.1 | async-start | bytes 131072 | tf_op jit(solution)/shard_map/while/body/eval_jaxpr/psum | solution.py:60
Sparse Core Ops, SparseCore 0:
  26.4 69.5 all-reduce.3
  112.8 69.3 all-reduce.3
  198.1 69.3 all-reduce.5
  283.4 69.3 all-reduce.5
where the time goes:
time: 403 us; the launch traced here: 402 us
  waiting for transfers between devices  278 us (69%)
  blocking collectives  80.2 us (20%)
  matrix products  20.8 us (5%)
  between operations  13.8 us (3%)
  local copies, waits for them, and re-layouts  4.26 us (1%)
  other arithmetic  4.03 us (1%)
    psum x4, waiting for transfers between devices, step(): piece = lax.psum(term, 'row')  278 us
    psum x4, blocking collectives, step(): summed = lax.psum(partial_value, 'col')  43 us
    psum x1, blocking collectives, local(): first, gram = lax.psum((local_first, herm_dot(basis, basis)), 'row')  37.1 us
    dot_general x52, matrix products, real_dot(): jnp.dot(left, right, preferred_element_type=jnp.float32, precision=lax.Pr...  20.8 us
  transfers between devices with their start and end apart: 4, of which 4 were waited for; matrix products, arithmetic and copies ran while one was open for 0% of the time, Pallas kernels for 0%

commit v1 on v0

v1 whole, which is shorter than its diff:
```python
import functools

import jax
import jax.numpy as jnp
from jax import lax
from jax.experimental import pallas as pl
from jax.experimental.pallas import tpu as pltpu
from jax.sharding import PartitionSpec as P

MESH = pl.DeviceIdType.MESH
F32 = jnp.float32
BF16 = jnp.bfloat16


def split(value):
    high = value.astype(BF16)
    low = (value - high.astype(F32)).astype(BF16)
    return high, low


def dot_nt(left, right):
    return lax.dot_general(left, right, (((1,), (1,)), ((), ())), preferred_element_type=F32)


def dot_nn(left, right):
    return lax.dot_general(left, right, (((1,), (0,)), ((), ())), preferred_element_type=F32)


def product(left, high, low, dot):
    rows = left.shape[0]
    left_high, left_low = split(left)
    both = dot(jnp.concatenate([left_high, left_low], 0), high)
    return both[:rows] + (both[rows:] + dot(left_high, low))


def complex_left(pieces, nvec):
    re = [x[:nvec] for x in pieces]
    im = [x[nvec:] for x in pieces]
    top = jnp.concatenate(re + [-x for x in im], 1)
    bottom = jnp.concatenate(im + re, 1)
    return jnp.concatenate([top, bottom], 0)


def kernel(
    R, C, factor, lower, upper, krylov, basis, projected, coefficients,
    inv_hi, inv_lo, fac_hi, fac_lo, bas_hi, bas_lo,
    psend, precv, ybuf, xbuf, bcast, vbuf, vrecv, fsend, frecv, gacc, grecv,
    psend_sem, precv_sem, bsend_sem, brecv_sem, vsend_sem, vrecv_sem, xsend_sem, xrecv_sem,
    fsend_sem, frecv_sem, gsend_sem, grecv_sem,
):
    tile, rows = lower.shape[1], lower.shape[2]
    width = factor.shape[2]
    nvec = krylov.shape[1]
    nb = basis.shape[1]
    share = tile // rows
    per = tile // width
    pieces = width // rows
    steps = R.bit_length() - 1
    r = lax.axis_index("row")
    c = lax.axis_index("col")
    t, p = r // share, r % share
    j, h = c // per, c % per
    solver = j == t

    barrier = pltpu.get_barrier_semaphore()

    def greet_row(i, carry):
        pl.semaphore_signal(barrier, inc=1, device_id=((r + 1 + i) % R, c), device_id_type=MESH)
        return carry

    def greet_col(i, carry):
        pl.semaphore_signal(barrier, inc=1, device_id=(r, (c + 1 + i) % C), device_id_type=MESH)
        return carry

    lax.fori_loop(0, R - 1, greet_row, 0)
    lax.fori_loop(0, C - 1, greet_col, 0)

    def prepare(ref, slot):
        high, low = split(jnp.concatenate([ref[0], ref[1]], 1))
        inv_hi[slot] = high
        inv_lo[slot] = low

    @pl.when(solver)
    def _():
        prepare(lower, 0)

    @pl.when(jnp.logical_not(solver))
    def _():
        high, low = split(jnp.concatenate([factor[0], factor[1]], 1))
        fac_hi[...] = high
        fac_lo[...] = low

    def prepare_basis():
        top = jnp.concatenate([basis[0], basis[1]], 1)
        bottom = jnp.concatenate([-basis[1], basis[0]], 1)
        high, low = split(jnp.concatenate([top, bottom], 0))
        bas_hi[...] = high
        bas_lo[...] = low
        gacc[0] = product(top, high, low, dot_nt)

    def remote(src, dst, send, recv, dest):
        return pltpu.make_async_remote_copy(
            src_ref=src, dst_ref=dst, send_sem=send, recv_sem=recv, device_id=dest, device_id_type=MESH
        )

    def gram_copy(i):
        other = r + (1 << i) * (1 - 2 * ((r // (1 << i)) % 2))
        return remote(gacc.at[i], grecv.at[i], gsend_sem.at[i], grecv_sem.at[i], (other, c))

    def gram_all():
        for i in range(steps):
            copy = gram_copy(i)
            copy.start()
            copy.wait_recv()
            gacc[i + 1] = gacc[i] + grecv[i]

    def part_copy(sweep, d):
        q = (p + d) % share
        return remote(
            psend.at[sweep, q], precv.at[sweep, p], psend_sem.at[sweep, q], precv_sem.at[sweep, p], (t * share + q, c)
        )

    def part_arrival(sweep, d):
        q = (p + d) % share
        return remote(
            psend.at[sweep, q], precv.at[sweep, q], psend_sem.at[sweep, q], precv_sem.at[sweep, q], (t * share + q, c)
        ), q

    def v_copy(hh):
        return remote(vbuf, vrecv.at[c], vsend_sem.at[hh], vrecv_sem.at[c], (r, t * per + hh))

    def v_sum(first_col, last_col, value):
        def body(cc, total):
            remote(vbuf, vrecv.at[cc], vsend_sem.at[0], vrecv_sem.at[cc], (r, cc)).wait_recv()
            return total - vrecv[cc]

        return lax.fori_loop(first_col, last_col, body, value)

    def solve(sweep, g):
        out = product(complex_left([g], nvec), inv_hi[sweep], inv_lo[sweep], dot_nt)
        for q in range(share):
            psend[sweep, q] = out[:, q * rows:(q + 1) * rows]
        for d in range(1, share):
            part_copy(sweep, d).start()
        total = psend[sweep, p]
        for d in range(1, share):
            arrival, q = part_arrival(sweep, d)
            arrival.wait_recv()
            total = total + precv[sweep, q]
        return total

    def b_copy(buf, rr):
        return remote(buf, bcast.at[p % pieces], bsend_sem.at[rr], brecv_sem.at[p % pieces], (rr, c))

    def each(first_index, last_index, act):
        def body(i, carry):
            act(i)
            return carry

        lax.fori_loop(first_index, last_index, body, 0)

    def x_copy(tt):
        cc = tt * per + h
        return remote(xbuf, xbuf, xsend_sem.at[tt], xrecv_sem.at[0], (r, cc))

    speaks = p // pieces == h

    @pl.when(jnp.logical_and(solver, t > 0))
    def _():
        prepare(upper, 1)

    @pl.when(j > 0)
    def _():
        prepare_basis()

    pl.semaphore_wait(barrier, R - 1 + C - 1)

    @pl.when(j > 0)
    def _():
        gram_all()

    @pl.when(solver)
    def _():
        b = jnp.concatenate([krylov[0], krylov[1]], 0)
        ybuf[...] = solve(0, v_sum(0, t * per, b))

        @pl.when(speaks)
        def _():
            each((t + 1) * share, R, lambda rr: b_copy(ybuf, rr).start())

        @pl.when(t == 0)
        def _():
            prepare(upper, 1)

    @pl.when(jnp.logical_not(solver))
    def _():
        got = []
        for i in range(pieces):
            remote(ybuf, bcast.at[i], bsend_sem.at[0], brecv_sem.at[i], (r, t * per)).wait_recv()
            got.append(bcast[i])
        vbuf[...] = product(complex_left(got, nvec), fac_hi[...], fac_lo[...], dot_nt)
        for hh in range(per):
            v_copy(hh).start()

    @pl.when(j == 0)
    def _():
        prepare_basis()
        gram_all()

    @pl.when(solver)
    def _():
        xbuf[...] = solve(1, v_sum((t + 1) * per, C, ybuf[...]))

        @pl.when(speaks)
        def _():
            each(0, t * share, lambda rr: b_copy(xbuf, rr).start())

        each(0, t, lambda tt: x_copy(tt).start())
        each(t + 1, C // per, lambda tt: x_copy(tt).start())

    @pl.when(jnp.logical_not(solver))
    def _():
        remote(ybuf, xbuf, xsend_sem.at[0], xrecv_sem.at[0], (r, t * per)).wait_recv()

    x = xbuf[...]
    wide = jnp.concatenate([x[:nvec], x[nvec:]], 1)
    fsend[...] = product(wide, bas_hi[...], bas_lo[...], dot_nt)

    def f_copy(d):
        return remote(fsend, frecv.at[r], fsend_sem.at[d], frecv_sem.at[r], ((r + d) % R, c))

    each(1, R, lambda d: f_copy(d).start())
    frecv[r] = fsend[...]

    def f_wait(d):
        q = (r + d) % R
        remote(fsend, frecv.at[q], fsend_sem.at[d], frecv_sem.at[q], (q, c)).wait_recv()

    each(1, R, f_wait)
    first = frecv[0]
    for i in range(1, R):
        first = first + frecv[i]
    top = gacc[steps]
    gram = jnp.concatenate([top, jnp.concatenate([-top[:, nb:], top[:, :nb]], 1)], 0)
    gram_hi, gram_lo = split(gram)
    second = first - product(first, gram_hi, gram_lo, dot_nt)
    coeffs = first + second
    result = wide - product(coeffs, bas_hi[...], bas_lo[...], dot_nn)
    projected[0] = result[:, :rows]
    projected[1] = result[:, rows:]
    turned = coeffs.T
    coefficients[0] = turned[:nb]
    coefficients[1] = turned[nb:]

    each(1, R, lambda d: f_copy(d).wait_send())
    for i in range(steps):
        gram_copy(i).wait_send()

    @pl.when(solver)
    def _():
        for sweep in range(2):
            for d in range(1, share):
                part_copy(sweep, d).wait_send()

        @pl.when(speaks)
        def _():
            each((t + 1) * share, R, lambda rr: b_copy(ybuf, rr).wait_send())
            each(0, t * share, lambda rr: b_copy(xbuf, rr).wait_send())

        each(0, t, lambda tt: x_copy(tt).wait_send())
        each(t + 1, C // per, lambda tt: x_copy(tt).wait_send())

    @pl.when(jnp.logical_not(solver))
    def _():
        for hh in range(per):
            v_copy(hh).wait_send()


def local(R, C, factor, lower, upper, krylov, basis):
    tile, rows = lower.shape[1], lower.shape[2]
    width = factor.shape[2]
    nvec, nb = krylov.shape[1], basis.shape[1]
    share, per, pieces = tile // rows, tile // width, width // rows
    steps = R.bit_length() - 1
    dma = pltpu.SemaphoreType.DMA
    vmem = pl.BlockSpec(memory_space=pltpu.VMEM)
    block = (2 * nvec, rows)
    return pl.pallas_call(
        functools.partial(kernel, R, C),
        out_shape=(
            jax.ShapeDtypeStruct(krylov.shape, F32),
            jax.ShapeDtypeStruct((2, nb, nvec), F32),
        ),
        in_specs=[vmem] * 5,
        out_specs=(vmem, vmem),
        scratch_shapes=[
            pltpu.VMEM((2, tile, 2 * rows), BF16),
            pltpu.VMEM((2, tile, 2 * rows), BF16),
            pltpu.VMEM((rows, 2 * width), BF16),
            pltpu.VMEM((rows, 2 * width), BF16),
            pltpu.VMEM((2 * nb, 2 * rows), BF16),
            pltpu.VMEM((2 * nb, 2 * rows), BF16),
            pltpu.VMEM((2, share) + block, F32),
            pltpu.VMEM((2, share) + block, F32),
            pltpu.VMEM(block, F32),
            pltpu.VMEM(block, F32),
            pltpu.VMEM((pieces,) + block, F32),
            pltpu.VMEM(block, F32),
            pltpu.VMEM((C,) + block, F32),
            pltpu.VMEM((nvec, 2 * nb), F32),
            pltpu.VMEM((R, nvec, 2 * nb), F32),
            pltpu.VMEM((steps + 1, nb, 2 * nb), F32),
            pltpu.VMEM((steps, nb, 2 * nb), F32),
            dma((2, share)),
            dma((2, share)),
            dma((R,)),
            dma((pieces,)),
            dma((per,)),
            dma((C,)),
            dma((C // per,)),
            dma((1,)),
            dma((R,)),
            dma((R,)),
            dma((steps,)),
            dma((steps,)),
        ],
        compiler_params=pltpu.CompilerParams(collective_id=0, has_side_effects=True),
        name="krylov_step",
    )(factor, lower, upper, krylov, basis)


def solution(mesh):
    in_specs = (
        P(None, "row", "col"),
        P(None, None, "row"),
        P(None, None, "row"),
        P(None, None, "row"),
        P(None, None, "row"),
    )
    out_specs = (P(None, None, "row"), P())
    body = functools.partial(local, mesh.shape["row"], mesh.shape["col"])
    return jax.shard_map(body, mesh=mesh, in_specs=in_specs, out_specs=out_specs, check_vma=False)
```

time: 403 us -> 43.3 us (0.11)
  the two profiles are of different devices: /device:TPU:0 before, /device:TPU:2 now
where the time goes in v1:
time: 43.3 us; the launch traced here: 43.1 us
  Pallas kernels  40.3 us (93%)
  local copies, waits for them, and re-layouts  2.13 us (5%)
  between operations  0.65 us (2%)
    pallas_call x1, Pallas kernels, local(): pl.pallas_call(functools.partial(kernel, R, C), out_shape=(jax.ShapeDtype...  40.3 us
    pallas_call x1, local copies, waits for them, and re-layouts, local(): pl.pallas_call(functools.partial(kernel, R, C), out_shape=(jax.ShapeDtype...  1.52 us

profile of v1, /device:TPU:2, one launch (start us, length us, event | category | flops | bytes accessed | tf_op | source)
XLA Modules:
  0.0 43.1 jit_solution(13754997593157658901)
XLA Ops:
  0.6 40.3 %krylov_step.1 = (f32[2,16,128]{2,1,0:T(8,128)}, f32[2,64,16]{2,1,0:T(8,128)}) custom-call(f32[2,128,256]{2,1,0:T(8,128)} %factor.1, f32[2,512,128]{2,1,0:T(8,128)} %lower.1, f32[2,512,128]{2,1,0:T(8,128)} %upper.1, f32[2,16,128]{2,1,0:T(8,128)} %krylov.1, f32[2,64,128]{2,1,0:T(8,128)} %basis.1), custom_call_target="tpu_custom_call" | custom-call | tf_op jit(solution)/shard_map/krylov_step/pallas_call | solution.py:288
  40.9 0.0 copy-start
  40.9 1.5 %copy.7 = f32[2,64,16]{1,2,0:T(8,128)} copy(f32[2,64,16]{2,1,0:T(8,128)} %get-tuple-element.3) | data formatting | bytes 16384 | tf_op jit(solution)/shard_map/krylov_step/pallas_call | solution.py:288
  42.5 0.0 copy-done
  42.5 0.6 %copy.9 = f32[2,16,128]{2,1,0:T(8,128)} copy(f32[2,16,128]{2,1,0:T(8,128)S(1)} %copy-done) | data formatting | bytes 32768
Async XLA Ops:
  40.9 1.5 %copy-start = (f32[2,16,128]{2,1,0:T(8,128)S(1)}, f32[2,16,128]{2,1,0:T(8,128)}, u32[]{:S(2)}) copy-start(f32[2,16,128]{2,1,0:T(8,128)} %get-tuple-element.6) | copy-start | bytes 49156

commit v2 on v1

--- a/solution.py
+++ b/solution.py
@@ -44,9 +44,10 @@
 def kernel(
     R, C, factor, lower, upper, krylov, basis, projected, coefficients,
     inv_hi, inv_lo, fac_hi, fac_lo, bas_hi, bas_lo,
+    end_hi, end_lo, lead_hi, lead_lo, gather,
     psend, precv, ybuf, xbuf, bcast, vbuf, vrecv, fsend, frecv, gacc, grecv,
     psend_sem, precv_sem, bsend_sem, brecv_sem, vsend_sem, vrecv_sem, xsend_sem, xrecv_sem,
-    fsend_sem, frecv_sem, gsend_sem, grecv_sem,
+    fsend_sem, frecv_sem, gsend_sem, grecv_sem, tsend_sem, trecv_sem, ysend_sem, yrecv_sem,
 ):
     tile, rows = lower.shape[1], lower.shape[2]
     width = factor.shape[2]
@@ -103,6 +104,13 @@
             src_ref=src, dst_ref=dst, send_sem=send, recv_sem=recv, device_id=dest, device_id_type=MESH
         )
 
+    def each(first_index, last_index, act):
+        def body(i, carry):
+            act(i)
+            return carry
+
+        lax.fori_loop(first_index, last_index, body, 0)
+
     def gram_copy(i):
         other = r + (1 << i) * (1 - 2 * ((r // (1 << i)) % 2))
         return remote(gacc.at[i], grecv.at[i], gsend_sem.at[i], grecv_sem.at[i], (other, c))
@@ -113,6 +121,50 @@
             copy.start()
             copy.wait_recv()
             gacc[i + 1] = gacc[i] + grecv[i]
+        top = gacc[steps]
+        gram = jnp.concatenate([top, jnp.concatenate([-top[:, nb:], top[:, :nb]], 1)], 0)
+        row_id = lax.broadcasted_iota(jnp.int32, gram.shape, 0)
+        col_id = lax.broadcasted_iota(jnp.int32, gram.shape, 1)
+        twice = jnp.where(row_id == col_id, 2.0, 0.0) - gram
+        spread = product(twice, bas_hi[...], bas_lo[...], dot_nn)
+        high, low = split(jnp.concatenate([twice, spread], 1))
+        end_hi[...] = high
+        end_lo[...] = low
+
+    def t_copy(d):
+        q = (p + d) % share
+        return remote(basis, gather.at[p], tsend_sem.at[d], trecv_sem.at[p], (t * share + q, c))
+
+    def lead_send():
+        for d in range(1, share):
+            t_copy(d).start()
+        gather[p] = basis[...]
+
+    def lead_all():
+        for d in range(1, share):
+            q = (p + d) % share
+            remote(basis, gather.at[q], tsend_sem.at[d], trecv_sem.at[q], (t * share + q, c)).wait_recv()
+        left = jnp.concatenate(
+            [jnp.concatenate([gather[q, i] for q in range(share)], 1) for i in range(2)], 0
+        )
+        out = product(left, inv_hi[1], inv_lo[1], dot_nn)
+        one = out[:nb, :rows] + out[nb:, rows:]
+        two = out[nb:, :rows] - out[:nb, rows:]
+        whole = jnp.concatenate([jnp.concatenate([one, two], 1), jnp.concatenate([-two, one], 1)], 0)
+        high, low = split(whole)
+        lead_hi[...] = high
+        lead_lo[...] = low
+
+    def side_work():
+        @pl.when(t == 0)
+        def _():
+            lead_send()
+
+        gram_all()
+
+        @pl.when(t == 0)
+        def _():
+            lead_all()
 
     def part_copy(sweep, d):
         q = (p + d) % share
@@ -126,15 +178,36 @@
             psend.at[sweep, q], precv.at[sweep, q], psend_sem.at[sweep, q], precv_sem.at[sweep, q], (t * share + q, c)
         ), q
 
-    def v_copy(hh):
-        return remote(vbuf, vrecv.at[c], vsend_sem.at[hh], vrecv_sem.at[c], (r, t * per + hh))
+    def v_copy(cc):
+        return remote(vbuf, vrecv.at[c], vsend_sem.at[cc], vrecv_sem.at[c], (r, cc))
+
+    def v_each(act):
+        @pl.when(t > 0)
+        def _():
+            for hh in range(per):
+                act(v_copy(t * per + hh))
+
+        @pl.when(t == 0)
+        def _():
+            each(1, C, lambda d: act(v_copy((c + d) % C)))
 
     def v_sum(first_col, last_col, value):
         def body(cc, total):
-            remote(vbuf, vrecv.at[cc], vsend_sem.at[0], vrecv_sem.at[cc], (r, cc)).wait_recv()
+            @pl.when(cc != c)
+            def _():
+                remote(vbuf, vrecv.at[cc], vsend_sem.at[0], vrecv_sem.at[cc], (r, cc)).wait_recv()
+
             return total - vrecv[cc]
 
         return lax.fori_loop(first_col, last_col, body, value)
+
+    def f_copy(d):
+        return remote(fsend, frecv.at[r], fsend_sem.at[d], frecv_sem.at[r], ((r + d) % R, c))
+
+    def send_first(value, high, low):
+        wide_value = jnp.concatenate([value[:nvec], value[nvec:]], 1)
+        fsend[...] = product(wide_value, high, low, dot_nt)
+        each(1, R, lambda d: f_copy(d).start())
 
     def solve(sweep, g):
         out = product(complex_left([g], nvec), inv_hi[sweep], inv_lo[sweep], dot_nt)
@@ -152,20 +225,16 @@
     def b_copy(buf, rr):
         return remote(buf, bcast.at[p % pieces], bsend_sem.at[rr], brecv_sem.at[p % pieces], (rr, c))
 
-    def each(first_index, last_index, act):
-        def body(i, carry):
-            act(i)
-            return carry
-
-        lax.fori_loop(first_index, last_index, body, 0)
-
     def x_copy(tt):
         cc = tt * per + h
         return remote(xbuf, xbuf, xsend_sem.at[tt], xrecv_sem.at[0], (r, cc))
 
+    def y_copy(tt):
+        return remote(ybuf, ybuf, ysend_sem.at[tt], yrecv_sem.at[0], (r, tt * per + h))
+
     speaks = p // pieces == h
 
-    @pl.when(jnp.logical_and(solver, t > 0))
+    @pl.when(solver != (t == 0))
     def _():
         prepare(upper, 1)
 
@@ -177,7 +246,7 @@
 
     @pl.when(j > 0)
     def _():
-        gram_all()
+        side_work()
 
     @pl.when(solver)
     def _():
@@ -190,6 +259,7 @@
 
         @pl.when(t == 0)
         def _():
+            each(1, C // per, lambda tt: y_copy(tt).start())
             prepare(upper, 1)
 
     @pl.when(jnp.logical_not(solver))
@@ -198,38 +268,45 @@
         for i in range(pieces):
             remote(ybuf, bcast.at[i], bsend_sem.at[0], brecv_sem.at[i], (r, t * per)).wait_recv()
             got.append(bcast[i])
-        vbuf[...] = product(complex_left(got, nvec), fac_hi[...], fac_lo[...], dot_nt)
-        for hh in range(per):
-            v_copy(hh).start()
+        value = product(complex_left(got, nvec), fac_hi[...], fac_lo[...], dot_nt)
+        vbuf[...] = value
+        v_each(lambda copy: copy.start())
+        vrecv[c] = value
 
     @pl.when(j == 0)
     def _():
         prepare_basis()
-        gram_all()
-
-    @pl.when(solver)
-    def _():
-        xbuf[...] = solve(1, v_sum((t + 1) * per, C, ybuf[...]))
-
-        @pl.when(speaks)
-        def _():
-            each(0, t * share, lambda rr: b_copy(xbuf, rr).start())
-
-        each(0, t, lambda tt: x_copy(tt).start())
-        each(t + 1, C // per, lambda tt: x_copy(tt).start())
-
-    @pl.when(jnp.logical_not(solver))
-    def _():
-        remote(ybuf, xbuf, xsend_sem.at[0], xrecv_sem.at[0], (r, t * per)).wait_recv()
-
-    x = xbuf[...]
-    wide = jnp.concatenate([x[:nvec], x[nvec:]], 1)
-    fsend[...] = product(wide, bas_hi[...], bas_lo[...], dot_nt)
-
-    def f_copy(d):
-        return remote(fsend, frecv.at[r], fsend_sem.at[d], frecv_sem.at[r], ((r + d) % R, c))
-
-    each(1, R, lambda d: f_copy(d).start())
+        side_work()
+
+    @pl.when(t == 0)
+    def _():
+        @pl.when(jnp.logical_not(solver))
+        def _():
+            remote(ybuf, ybuf, ysend_sem.at[0], yrecv_sem.at[0], (r, h)).wait_recv()
+
+        g = v_sum(per, C, ybuf[...])
+        send_first(g, lead_hi[...], lead_lo[...])
+        xbuf[...] = solve(1, g)
+
+    @pl.when(t > 0)
+    def _():
+        @pl.when(solver)
+        def _():
+            xbuf[...] = solve(1, v_sum((t + 1) * per, C, ybuf[...]))
+
+            @pl.when(speaks)
+            def _():
+                each(0, t * share, lambda rr: b_copy(xbuf, rr).start())
+
+            each(0, t, lambda tt: x_copy(tt).start())
+            each(t + 1, C // per, lambda tt: x_copy(tt).start())
+
+        @pl.when(jnp.logical_not(solver))
+        def _():
+            remote(ybuf, xbuf, xsend_sem.at[0], xrecv_sem.at[0], (r, t * per)).wait_recv()
+
+        send_first(xbuf[...], bas_hi[...], bas_lo[...])
+
     frecv[r] = fsend[...]
 
     def f_wait(d):
@@ -240,40 +317,52 @@
     first = frecv[0]
     for i in range(1, R):
         first = first + frecv[i]
-    top = gacc[steps]
-    gram = jnp.concatenate([top, jnp.concatenate([-top[:, nb:], top[:, :nb]], 1)], 0)
-    gram_hi, gram_lo = split(gram)
-    second = first - product(first, gram_hi, gram_lo, dot_nt)
-    coeffs = first + second
-    result = wide - product(coeffs, bas_hi[...], bas_lo[...], dot_nn)
-    projected[0] = result[:, :rows]
-    projected[1] = result[:, rows:]
-    turned = coeffs.T
-    coefficients[0] = turned[:nb]
-    coefficients[1] = turned[nb:]
+    ends = product(first, end_hi[...], end_lo[...], dot_nn)
+    coefficients[0] = ends[:, :nb]
+    coefficients[1] = ends[:, nb:2 * nb]
+    projected[0] = xbuf[:nvec] - ends[:, 2 * nb:2 * nb + rows]
+    projected[1] = xbuf[nvec:] - ends[:, 2 * nb + rows:]
 
     each(1, R, lambda d: f_copy(d).wait_send())
     for i in range(steps):
         gram_copy(i).wait_send()
 
+    def parts_sent(sweep):
+        for d in range(1, share):
+            part_copy(sweep, d).wait_send()
+
+    @pl.when(t == 0)
+    def _():
+        parts_sent(1)
+        for d in range(1, share):
+            t_copy(d).wait_send()
+
     @pl.when(solver)
     def _():
-        for sweep in range(2):
-            for d in range(1, share):
-                part_copy(sweep, d).wait_send()
+        parts_sent(0)
 
         @pl.when(speaks)
         def _():
             each((t + 1) * share, R, lambda rr: b_copy(ybuf, rr).wait_send())
-            each(0, t * share, lambda rr: b_copy(xbuf, rr).wait_send())
-
-        each(0, t, lambda tt: x_copy(tt).wait_send())
-        each(t + 1, C // per, lambda tt: x_copy(tt).wait_send())
+
+        @pl.when(t == 0)
+        def _():
+            each(1, C // per, lambda tt: y_copy(tt).wait_send())
+
+        @pl.when(t > 0)
+        def _():
+            parts_sent(1)
+
+            @pl.when(speaks)
+            def _():
+                each(0, t * share, lambda rr: b_copy(xbuf, rr).wait_send())
+
+            each(0, t, lambda tt: x_copy(tt).wait_send())
+            each(t + 1, C // per, lambda tt: x_copy(tt).wait_send())
 
     @pl.when(jnp.logical_not(solver))
     def _():
-        for hh in range(per):
-            v_copy(hh).wait_send()
+        v_each(lambda copy: copy.wait_send())
 
 
 def local(R, C, factor, lower, upper, krylov, basis):
@@ -285,11 +374,11 @@
     dma = pltpu.SemaphoreType.DMA
     vmem = pl.BlockSpec(memory_space=pltpu.VMEM)
     block = (2 * nvec, rows)
-    return pl.pallas_call(
+    projected, turned = pl.pallas_call(
         functools.partial(kernel, R, C),
         out_shape=(
             jax.ShapeDtypeStruct(krylov.shape, F32),
-            jax.ShapeDtypeStruct((2, nb, nvec), F32),
+            jax.ShapeDtypeStruct((2, nvec, nb), F32),
         ),
         in_specs=[vmem] * 5,
         out_specs=(vmem, vmem),
@@ -300,6 +389,11 @@
             pltpu.VMEM((rows, 2 * width), BF16),
             pltpu.VMEM((2 * nb, 2 * rows), BF16),
             pltpu.VMEM((2 * nb, 2 * rows), BF16),
+            pltpu.VMEM((2 * nb, 2 * nb + 2 * rows), BF16),
+            pltpu.VMEM((2 * nb, 2 * nb + 2 * rows), BF16),
+            pltpu.VMEM((2 * nb, 2 * rows), BF16),
+            pltpu.VMEM((2 * nb, 2 * rows), BF16),
+            pltpu.VMEM((share, 2, nb, rows), F32),
             pltpu.VMEM((2, share) + block, F32),
             pltpu.VMEM((2, share) + block, F32),
             pltpu.VMEM(block, F32),
@@ -315,7 +409,7 @@
             dma((2, share)),
             dma((R,)),
             dma((pieces,)),
-            dma((per,)),
+            dma((C,)),
             dma((C,)),
             dma((C // per,)),
             dma((1,)),
@@ -323,10 +417,15 @@
             dma((R,)),
             dma((steps,)),
             dma((steps,)),
+            dma((share,)),
+            dma((share,)),
+            dma((C // per,)),
+            dma((1,)),
         ],
         compiler_params=pltpu.CompilerParams(collective_id=0, has_side_effects=True),
         name="krylov_step",
     )(factor, lower, upper, krylov, basis)
+    return projected, turned.transpose(0, 2, 1)
 
 
 def solution(mesh):

time: 43.3 us -> 40.8 us (0.942)
  the two profiles are of different devices: /device:TPU:2 before, /device:TPU:0 now
where the time goes in v2:
time: 40.8 us; the launch traced here: 40.6 us
  Pallas kernels  38 us (93%)
  local copies, waits for them, and re-layouts  1.94 us (5%)
  between operations  0.65 us (2%)
    pallas_call x1, Pallas kernels, local(): pl.pallas_call(functools.partial(kernel, R, C), out_shape=(jax.ShapeDtype...  38 us
    unnamed x4, local copies, waits for them, and re-layouts  1.94 us

profile of v2, /device:TPU:0, one launch (start us, length us, event | category | flops | bytes accessed | tf_op | source)
XLA Modules:
  0.0 40.6 jit_solution(3993876770029983974)
XLA Ops:
  0.6 38.0 %krylov_step.1 = (f32[2,16,128]{2,1,0:T(8,128)}, f32[2,16,64]{2,1,0:T(8,128)}) custom-call(f32[2,128,256]{2,1,0:T(8,128)} %factor.1, f32[2,512,128]{2,1,0:T(8,128)} %lower.1, f32[2,512,128]{2,1,0:T(8,128)} %upper.1, f32[2,16,128]{2,1,0:T(8,128)} %krylov.1, f32[2,64,128]{2,1,0:T(8,128)} %basis.1), custom_call_target="tpu_custom_call" | custom-call | tf_op jit(solution)/shard_map/krylov_step/pallas_call | solution.py:377
  38.7 0.0 copy-start
  38.7 1.3 %copy.9 = f32[2,16,128]{2,1,0:T(8,128)} copy(f32[2,16,128]{2,1,0:T(8,128)} %get-tuple-element.8) | data formatting | bytes 32768
  40.0 0.0 copy-done
  40.0 0.6 %copy.10 = f32[2,64,16]{1,2,0:T(8,128)} copy(f32[2,64,16]{1,2,0:T(8,128)S(1)} %bitcast.1) | data formatting | bytes 16384
Async XLA Ops:
  38.7 1.3 %copy-start = (f32[2,16,64]{2,1,0:T(8,128)S(1)}, f32[2,16,64]{2,1,0:T(8,128)}, u32[]{:S(2)}) copy-start(f32[2,16,64]{2,1,0:T(8,128)} %get-tuple-element.5) | copy-start | bytes 24580

commit v3 on v2

--- a/solution.py
+++ b/solution.py
@@ -44,10 +44,11 @@
 def kernel(
     R, C, factor, lower, upper, krylov, basis, projected, coefficients,
     inv_hi, inv_lo, fac_hi, fac_lo, bas_hi, bas_lo,
-    end_hi, end_lo, lead_hi, lead_lo, gather,
+    end_hi, end_lo, lead_hi, lead_lo, gather, both_hi, both_lo, slab,
     psend, precv, ybuf, xbuf, bcast, vbuf, vrecv, fsend, frecv, gacc, grecv,
     psend_sem, precv_sem, bsend_sem, brecv_sem, vsend_sem, vrecv_sem, xsend_sem, xrecv_sem,
     fsend_sem, frecv_sem, gsend_sem, grecv_sem, tsend_sem, trecv_sem, ysend_sem, yrecv_sem,
+    usend_sem, urecv_sem, zsend_sem,
 ):
     tile, rows = lower.shape[1], lower.shape[2]
     width = factor.shape[2]
@@ -62,6 +63,7 @@
     t, p = r // share, r % share
     j, h = c // per, c % per
     solver = j == t
+    last = jnp.logical_and(solver, t == C // per - 1)
 
     barrier = pltpu.get_barrier_semaphore()
 
@@ -155,6 +157,31 @@
         lead_hi[...] = high
         lead_lo[...] = low
 
+    def u_copy(d):
+        q = (p + d) % share
+        source = upper.at[:, pl.ds(pl.multiple_of(h * width, width), width), :]
+        return remote(source, slab.at[p], usend_sem.at[d], urecv_sem.at[p], (t * share + q, c))
+
+    def both_all():
+        for d in range(1, share):
+            q = (p + d) % share
+            remote(slab.at[p], slab.at[q], usend_sem.at[d], urecv_sem.at[q], (t * share + q, c)).wait_recv()
+        slab[p] = upper[:, pl.ds(pl.multiple_of(h * width, width), width), :]
+        for i in range(pieces):
+            left = jnp.concatenate(
+                [
+                    jnp.concatenate([slab[q, k, i * rows:(i + 1) * rows, :] for q in range(share)], 1)
+                    for k in range(2)
+                ],
+                0,
+            )
+            out = product(left, inv_hi[0], inv_lo[0], dot_nn)
+            re = out[:rows, :rows] - out[rows:, rows:]
+            im = out[:rows, rows:] + out[rows:, :rows]
+            high, low = split(jnp.concatenate([re, im], 1))
+            both_hi[i * rows:(i + 1) * rows, :] = high
+            both_lo[i * rows:(i + 1) * rows, :] = low
+
     def side_work():
         @pl.when(t == 0)
         def _():
@@ -222,6 +249,25 @@
             total = total + precv[sweep, q]
         return total
 
+    def w_copy(i):
+        q = h * pieces + i
+        return remote(
+            psend.at[0, q], precv.at[0, p], psend_sem.at[0, q], precv_sem.at[0, p], (t * share + q, c)
+        )
+
+    def w_each(act):
+        for i in range(pieces):
+
+            @pl.when(h * pieces + i != p)
+            def _(i=i):
+                act(w_copy(i))
+
+    def w_solve(g):
+        out = product(complex_left([g], nvec), both_hi[...], both_lo[...], dot_nt)
+        for i in range(pieces):
+            psend[0, h * pieces + i] = out[:, i * rows:(i + 1) * rows]
+        w_each(lambda copy: copy.start())
+
     def b_copy(buf, rr):
         return remote(buf, bcast.at[p % pieces], bsend_sem.at[rr], brecv_sem.at[p % pieces], (rr, c))
 
@@ -229,12 +275,15 @@
         cc = tt * per + h
         return remote(xbuf, xbuf, xsend_sem.at[tt], xrecv_sem.at[0], (r, cc))
 
+    def z_copy(d):
+        return remote(xbuf, xbuf, zsend_sem.at[d], xrecv_sem.at[0], (r, (c + d) % C))
+
     def y_copy(tt):
         return remote(ybuf, ybuf, ysend_sem.at[tt], yrecv_sem.at[0], (r, tt * per + h))
 
     speaks = p // pieces == h
 
-    @pl.when(solver != (t == 0))
+    @pl.when(jnp.logical_and(solver != (t == 0), jnp.logical_not(last)))
     def _():
         prepare(upper, 1)
 
@@ -244,11 +293,33 @@
 
     pl.semaphore_wait(barrier, R - 1 + C - 1)
 
+    @pl.when(last)
+    def _():
+        for d in range(1, share):
+            u_copy(d).start()
+
     @pl.when(j > 0)
     def _():
         side_work()
 
-    @pl.when(solver)
+    @pl.when(last)
+    def _():
+        both_all()
+        b = jnp.concatenate([krylov[0], krylov[1]], 0)
+        w_solve(v_sum(0, t * per, b))
+
+        @pl.when(speaks)
+        def _():
+            total = psend[0, p]
+            for d in range(1, share):
+                arrival, q = part_arrival(0, d)
+                arrival.wait_recv()
+                total = total + precv[0, q]
+            xbuf[...] = total
+            each(0, t * share, lambda rr: b_copy(xbuf, rr).start())
+            each(1, C, lambda d: z_copy(d).start())
+
+    @pl.when(jnp.logical_and(solver, jnp.logical_not(last)))
     def _():
         b = jnp.concatenate([krylov[0], krylov[1]], 0)
         ybuf[...] = solve(0, v_sum(0, t * per, b))
@@ -290,7 +361,7 @@
 
     @pl.when(t > 0)
     def _():
-        @pl.when(solver)
+        @pl.when(jnp.logical_and(solver, jnp.logical_not(last)))
         def _():
             xbuf[...] = solve(1, v_sum((t + 1) * per, C, ybuf[...]))
 
@@ -301,7 +372,7 @@
             each(0, t, lambda tt: x_copy(tt).start())
             each(t + 1, C // per, lambda tt: x_copy(tt).start())
 
-        @pl.when(jnp.logical_not(solver))
+        @pl.when(jnp.logical_not(jnp.logical_and(solver, jnp.logical_or(speaks, jnp.logical_not(last)))))
         def _():
             remote(ybuf, xbuf, xsend_sem.at[0], xrecv_sem.at[0], (r, t * per)).wait_recv()
 
@@ -337,7 +408,18 @@
         for d in range(1, share):
             t_copy(d).wait_send()
 
-    @pl.when(solver)
+    @pl.when(last)
+    def _():
+        for d in range(1, share):
+            u_copy(d).wait_send()
+        w_each(lambda copy: copy.wait_send())
+
+        @pl.when(speaks)
+        def _():
+            each(0, t * share, lambda rr: b_copy(xbuf, rr).wait_send())
+            each(1, C, lambda d: z_copy(d).wait_send())
+
+    @pl.when(jnp.logical_and(solver, jnp.logical_not(last)))
     def _():
         parts_sent(0)
 
@@ -394,6 +476,9 @@
             pltpu.VMEM((2 * nb, 2 * rows), BF16),
             pltpu.VMEM((2 * nb, 2 * rows), BF16),
             pltpu.VMEM((share, 2, nb, rows), F32),
+            pltpu.VMEM((width, 2 * rows), BF16),
+            pltpu.VMEM((width, 2 * rows), BF16),
+            pltpu.VMEM((share, 2, width, rows), F32),
             pltpu.VMEM((2, share) + block, F32),
             pltpu.VMEM((2, share) + block, F32),
             pltpu.VMEM(block, F32),
@@ -421,6 +506,9 @@
             dma((share,)),
             dma((C // per,)),
             dma((1,)),
+            dma((share,)),
+            dma((share,)),
+            dma((C,)),
         ],
         compiler_params=pltpu.CompilerParams(collective_id=0, has_side_effects=True),
         name="krylov_step",

time: 40.8 us -> 42.1 us (1.032)
  Pallas kernels: 38 us -> 39.4 us
    pallas_call x1, Pallas kernels: 38 us -> 39.4 us  [local(): pl.pallas_call(functools.partial(kernel, R, C), out_shape=(jax.ShapeDtype...]
where the time goes in v3:
time: 42.1 us; the launch traced here: 42 us
  Pallas kernels  39.4 us (94%)
  local copies, waits for them, and re-layouts  1.94 us (5%)
  between operations  0.65 us (2%)
    pallas_call x1, Pallas kernels, local(): pl.pallas_call(functools.partial(kernel, R, C), out_shape=(jax.ShapeDtype...  39.4 us
    unnamed x4, local copies, waits for them, and re-layouts  1.94 us

profile of v3, /device:TPU:0, one launch (start us, length us, event | category | flops | bytes accessed | tf_op | source)
XLA Modules:
  0.0 42.0 jit_solution(691588221654478652)
XLA Ops:
  0.6 39.4 %krylov_step.1 = (f32[2,16,128]{2,1,0:T(8,128)}, f32[2,16,64]{2,1,0:T(8,128)}) custom-call(f32[2,128,256]{2,1,0:T(8,128)} %factor.1, f32[2,512,128]{2,1,0:T(8,128)} %lower.1, f32[2,512,128]{2,1,0:T(8,128)} %upper.1, f32[2,16,128]{2,1,0:T(8,128)} %krylov.1, f32[2,64,128]{2,1,0:T(8,128)} %basis.1), custom_call_target="tpu_custom_call" | custom-call | tf_op jit(solution)/shard_map/krylov_step/pallas_call | solution.py:459
  40.0 0.0 copy-start
  40.0 1.3 %copy.9 = f32[2,16,128]{2,1,0:T(8,128)} copy(f32[2,16,128]{2,1,0:T(8,128)} %get-tuple-element.8) | data formatting | bytes 32768
  41.3 0.0 copy-done
  41.3 0.6 %copy.10 = f32[2,64,16]{1,2,0:T(8,128)} copy(f32[2,64,16]{1,2,0:T(8,128)S(1)} %bitcast.1) | data formatting | bytes 16384
Async XLA Ops:
  40.0 1.3 %copy-start = (f32[2,16,64]{2,1,0:T(8,128)S(1)}, f32[2,16,64]{2,1,0:T(8,128)}, u32[]{:S(2)}) copy-start(f32[2,16,64]{2,1,0:T(8,128)} %get-tuple-element.5) | copy-start | bytes 24580

commit v4 on v2

--- a/solution.py
+++ b/solution.py
@@ -156,14 +156,11 @@
         lead_lo[...] = low
 
     def side_work():
+        gram_all()
+
         @pl.when(t == 0)
         def _():
             lead_send()
-
-        gram_all()
-
-        @pl.when(t == 0)
-        def _():
             lead_all()
 
     def part_copy(sweep, d):
@@ -209,10 +206,16 @@
         fsend[...] = product(wide_value, high, low, dot_nt)
         each(1, R, lambda d: f_copy(d).start())
 
-    def solve(sweep, g):
+    def multiply(sweep, g):
         out = product(complex_left([g], nvec), inv_hi[sweep], inv_lo[sweep], dot_nt)
         for q in range(share):
             psend[sweep, q] = out[:, q * rows:(q + 1) * rows]
+
+    def solve(sweep, g):
+        multiply(sweep, g)
+        return exchange(sweep)
+
+    def exchange(sweep):
         for d in range(1, share):
             part_copy(sweep, d).start()
         total = psend[sweep, p]
@@ -242,6 +245,10 @@
     def _():
         prepare_basis()
 
+    @pl.when(jnp.logical_and(solver, t == 0))
+    def _():
+        multiply(0, jnp.concatenate([krylov[0], krylov[1]], 0))
+
     pl.semaphore_wait(barrier, R - 1 + C - 1)
 
     @pl.when(j > 0)
@@ -250,8 +257,12 @@
 
     @pl.when(solver)
     def _():
-        b = jnp.concatenate([krylov[0], krylov[1]], 0)
-        ybuf[...] = solve(0, v_sum(0, t * per, b))
+        @pl.when(t > 0)
+        def _():
+            b = jnp.concatenate([krylov[0], krylov[1]], 0)
+            multiply(0, v_sum(0, t * per, b))
+
+        ybuf[...] = exchange(0)
 
         @pl.when(speaks)
         def _():
@@ -363,6 +374,11 @@
     @pl.when(jnp.logical_not(solver))
     def _():
         v_each(lambda copy: copy.wait_send())
+
+
+def finish(projected, turned, projected_out, turned_out):
+    projected_out[...] = projected[...]
+    turned_out[...] = turned[...]
 
 
 def local(R, C, factor, lower, upper, krylov, basis):
@@ -425,6 +441,13 @@
         compiler_params=pltpu.CompilerParams(collective_id=0, has_side_effects=True),
         name="krylov_step",
     )(factor, lower, upper, krylov, basis)
+    projected, turned = pl.pallas_call(
+        finish,
+        out_shape=(jax.ShapeDtypeStruct(projected.shape, F32), jax.ShapeDtypeStruct(turned.shape, F32)),
+        in_specs=[vmem] * 2,
+        out_specs=(vmem, vmem),
+        name="finish",
+    )(projected, turned)
     return projected, turned.transpose(0, 2, 1)
 
 

time: 40.8 us -> 38.7 us (0.949)
  local copies, waits for them, and re-layouts: 1.94 us -> 0 us
    unnamed x4 -> x0, local copies, waits for them, and re-layouts: 1.94 us -> none
    pallas_call x1, Pallas kernels: 38 us -> 36.5 us  [local(): pl.pallas_call(functools.partial(kernel, R, C), out_shape=(jax.ShapeDtype...]
    pallas_call x0 -> x1, Pallas kernels: none -> 1.35 us  [local(): pl.pallas_call(finish, out_shape=(jax.ShapeDtypeStruct(projected.shape, F...]
where the time goes in v4:
time: 38.7 us; the launch traced here: 38.5 us
  Pallas kernels  37.8 us (98%)
  between operations  0.64 us (2%)
    pallas_call x1, Pallas kernels, local(): pl.pallas_call(functools.partial(kernel, R, C), out_shape=(jax.ShapeDtype...  36.5 us
    pallas_call x1, Pallas kernels, local(): pl.pallas_call(finish, out_shape=(jax.ShapeDtypeStruct(projected.shape, F...  1.35 us

profile of v4, /device:TPU:0, one launch (start us, length us, event | category | flops | bytes accessed | tf_op | source)
XLA Modules:
  0.0 38.5 jit_solution(789659430219798381)
XLA Ops:
  0.6 36.5 %krylov_step.1 = (f32[2,16,128]{2,1,0:T(8,128)}, f32[2,16,64]{2,1,0:T(8,128)}) custom-call(f32[2,128,256]{2,1,0:T(8,128)} %factor.1, f32[2,512,128]{2,1,0:T(8,128)} %lower.1, f32[2,512,128]{2,1,0:T(8,128)} %upper.1, f32[2,16,128]{2,1,0:T(8,128)} %krylov.1, f32[2,64,128]{2,1,0:T(8,128)} %basis.1), custom_call_target="tpu_custom_call" | custom-call | tf_op jit(solution)/shard_map/krylov_step/pallas_call | solution.py:393
  37.1 1.3 %finish.1 = (f32[2,16,128]{2,1,0:T(8,128)}, f32[2,16,64]{2,1,0:T(8,128)}) custom-call(f32[2,16,128]{2,1,0:T(8,128)} %get-tuple-element.6.projected, f32[2,16,64]{2,1,0:T(8,128)} %get-tuple-element.7.turned), custom_call_target="tpu_custom_call" | custom-call | tf_op jit(solution)/shard_map/finish/pallas_call | solution.py:444

commit v5 on v4

--- a/solution.py
+++ b/solution.py
@@ -48,6 +48,7 @@
     psend, precv, ybuf, xbuf, bcast, vbuf, vrecv, fsend, frecv, gacc, grecv,
     psend_sem, precv_sem, bsend_sem, brecv_sem, vsend_sem, vrecv_sem, xsend_sem, xrecv_sem,
     fsend_sem, frecv_sem, gsend_sem, grecv_sem, tsend_sem, trecv_sem, ysend_sem, yrecv_sem,
+    ready_sem,
 ):
     tile, rows = lower.shape[1], lower.shape[2]
     width = factor.shape[2]
@@ -65,15 +66,20 @@
 
     barrier = pltpu.get_barrier_semaphore()
 
-    def greet_row(i, carry):
-        pl.semaphore_signal(barrier, inc=1, device_id=((r + 1 + i) % R, c), device_id_type=MESH)
+    def greet_mate(i, carry):
+        pl.semaphore_signal(barrier, inc=1, device_id=(t * share + (p + 1 + i) % share, c), device_id_type=MESH)
+        return carry
+
+    def greet_tile(i, carry):
+        pl.semaphore_signal(barrier, inc=1, device_id=((r + (1 + i) * share) % R, c), device_id_type=MESH)
         return carry
 
     def greet_col(i, carry):
         pl.semaphore_signal(barrier, inc=1, device_id=(r, (c + 1 + i) % C), device_id_type=MESH)
         return carry
 
-    lax.fori_loop(0, R - 1, greet_row, 0)
+    lax.fori_loop(0, share - 1, greet_mate, 0)
+    lax.fori_loop(0, R // share - 1, greet_tile, 0)
     lax.fori_loop(0, C - 1, greet_col, 0)
 
     def prepare(ref, slot):
@@ -249,7 +255,11 @@
     def _():
         multiply(0, jnp.concatenate([krylov[0], krylov[1]], 0))
 
-    pl.semaphore_wait(barrier, R - 1 + C - 1)
+    pl.semaphore_wait(barrier, share - 1 + R // share - 1 + C - 1)
+    for d in range(1, share):
+        pl.semaphore_signal(
+            ready_sem, inc=1, device_id=(t * share + (p + d) % share, c), device_id_type=MESH
+        )
 
     @pl.when(j > 0)
     def _():
@@ -263,6 +273,7 @@
             multiply(0, v_sum(0, t * per, b))
 
         ybuf[...] = exchange(0)
+        pl.semaphore_wait(ready_sem, share - 1)
 
         @pl.when(speaks)
         def _():
@@ -275,6 +286,7 @@
 
     @pl.when(jnp.logical_not(solver))
     def _():
+        pl.semaphore_wait(ready_sem, share - 1)
         got = []
         for i in range(pieces):
             remote(ybuf, bcast.at[i], bsend_sem.at[0], brecv_sem.at[i], (r, t * per)).wait_recv()
@@ -437,6 +449,7 @@
             dma((share,)),
             dma((C // per,)),
             dma((1,)),
+            pltpu.SemaphoreType.REGULAR,
         ],
         compiler_params=pltpu.CompilerParams(collective_id=0, has_side_effects=True),
         name="krylov_step",

time: 38.7 us -> 38.1 us (0.984)
  Pallas kernels: 37.8 us -> 37.3 us
    pallas_call x1, Pallas kernels: 36.5 us -> 35.9 us  [local(): pl.pallas_call(functools.partial(kernel, R, C), out_shape=(jax.ShapeDtype...]
where the time goes in v5:
time: 38.1 us; the launch traced here: 37.9 us
  Pallas kernels  37.3 us (98%)
  between operations  0.64 us (2%)
    pallas_call x1, Pallas kernels, local(): pl.pallas_call(functools.partial(kernel, R, C), out_shape=(jax.ShapeDtype...  35.9 us
    pallas_call x1, Pallas kernels, local(): pl.pallas_call(finish, out_shape=(jax.ShapeDtypeStruct(projected.shape, F...  1.35 us

profile of v5, /device:TPU:0, one launch (start us, length us, event | category | flops | bytes accessed | tf_op | source)
XLA Modules:
  0.0 37.9 jit_solution(8263793176259493580)
XLA Ops:
  0.6 35.9 %krylov_step.1 = (f32[2,16,128]{2,1,0:T(8,128)}, f32[2,16,64]{2,1,0:T(8,128)}) custom-call(f32[2,128,256]{2,1,0:T(8,128)} %factor.1, f32[2,512,128]{2,1,0:T(8,128)} %lower.1, f32[2,512,128]{2,1,0:T(8,128)} %upper.1, f32[2,16,128]{2,1,0:T(8,128)} %krylov.1, f32[2,64,128]{2,1,0:T(8,128)} %basis.1), custom_call_target="tpu_custom_call" | custom-call | tf_op jit(solution)/shard_map/krylov_step/pallas_call | solution.py:405
  36.6 1.3 %finish.1 = (f32[2,16,128]{2,1,0:T(8,128)}, f32[2,16,64]{2,1,0:T(8,128)}) custom-call(f32[2,16,128]{2,1,0:T(8,128)} %get-tuple-element.6.projected, f32[2,16,64]{2,1,0:T(8,128)} %get-tuple-element.7.turned), custom_call_target="tpu_custom_call" | custom-call | tf_op jit(solution)/shard_map/finish/pallas_call | solution.py:457
